TPU v7x, 256 devices: a whole 4x4x8 slice. The times are simulated.
256 devices in a mesh: section: 16 (over x, z_hi), dp: 16 (over z_lo, y, core).
Axes of the slice: x: 4, y: 4, z: 8 (z_hi: 4, z_lo: 2; z = z_hi * 2 + z_lo), core: 2. Of those that a mesh axis runs over, the one named last changes fastest.
Arguments:
- section_inputs: bfloat16 [16, 768, 1152], P('section'), may hold values from -6 to 6
- mirror_held: bfloat16 [16, 768, 1152], P('section'), may hold values from -6 to 6
- section_cotangents: bfloat16 [16, 768, 1152], P('section'), may hold values from -6 to 6
- next_batch: bfloat16 [768, 1152], replicated, may hold values from -6 to 6
- loss_cotangent: bfloat16 [768, 1152], replicated, may hold values from -6 to 6
- join_weights: bfloat16 [16, 1152, 1152], P('section'), may hold values from -0.125 to 0.125
Outputs:
- section_outputs: bfloat16 [256, 2, 768, 1152], P(('dp', 'section')), parts along dimension 0
- section_gradients: bfloat16 [256, 2, 768, 1152], P(('dp', 'section')), parts along dimension 0
- mirror_arrivals: bfloat16 [256, 768, 1152], P(('dp', 'section')), parts along dimension 0
There are 16 independent parts, one for each index of `dp`. A program takes and returns all parts, laid end to end along the dimension named above; an argument that names none is the same for every part. Nothing has to cross between parts.
All inputs are finite; a program needn't handle non-finite values.
Results may differ from a plain program's by a relative error of at most 0.001.
Values may be sent and summed in bfloat16 or wider, within the bound.
No kernel may reach another device: no remote copies, remote signals or barrier semaphores. Data moves between devices by JAX's collectives and lax.ppermute only.
A program may use at most 128 MiB of HBM per device.

v0:
```python
import jax
import jax.numpy as jnp
from jax import lax
from jax.sharding import PartitionSpec as P


def relay_pairs(count):
    order = list(range(0, count, 2)) + list(range(count - 1, 0, -2))
    return list(zip(order[:-1], order[1:]))


def local(
    section_inputs, mirror_held, section_cotangents, next_batch, loss_cotangent, join_weights
):
    count = lax.axis_size("section")
    replicas = lax.axis_size("dp")
    position = lax.axis_index("section")
    is_early = position % 2 == 0
    weights = join_weights[0]
    rows = next_batch.shape[0] // replicas
    start = lax.axis_index("dp") * rows
    ahead = relay_pairs(count)
    back = [(b, a) for a, b in ahead]
    mirror = [(i, i ^ 1) for i in range(count)]

    def times(left):
        return jnp.dot(left, weights, preferred_element_type=jnp.float32)

    def times_t(left):
        return lax.dot_general(
            left, weights, (((1,), (1,)), ((), ())), preferred_element_type=jnp.float32
        )

    def forward(arriving, pending):
        product = times(arriving)
        joined = (product + pending.astype(jnp.float32)).astype(jnp.bfloat16)
        return (jnp.where(is_early, arriving, joined), product.astype(jnp.bfloat16))

    def backward(cotangent, returned):
        product = times_t(jnp.where(is_early, returned, cotangent))
        return jnp.where(is_early, cotangent.astype(jnp.float32) + product, product).astype(
            jnp.bfloat16
        )

    def part(whole):
        return lax.dynamic_slice_in_dim(whole, start, rows, 0)

    a, held, cot = (section_inputs[0], mirror_held[0], section_cotangents[0])
    a_part, held_part, cot_part = (part(a), part(held), part(cot))
    out_part, skip_part = forward(a_part, held_part)
    grad_part = backward(cot_part, held_part)
    came_out = lax.ppermute(out_part, "section", ahead)
    came_grad = lax.ppermute(grad_part, "section", back)
    came_mirror = lax.ppermute(jnp.where(is_early, skip_part, cot_part), "section", mirror)
    second_in = jnp.where(position == 0, part(next_batch), came_out)
    second_cot = jnp.where(position == 1, part(loss_cotangent), came_grad)
    second_out, second_skip = forward(second_in, came_mirror)
    second_grad = backward(second_cot, came_mirror)
    arrived = lax.ppermute(jnp.where(is_early, second_skip, second_cot), "section", mirror)
    parts = jnp.stack([second_out, second_grad, arrived], axis=0)
    whole = lax.all_gather(parts, "dp", axis=1, tiled=True)
    first_out, _ = forward(a, held)
    first_grad = backward(cot, held)
    section_outputs = jnp.stack([first_out, whole[0]], axis=0)[None]
    section_gradients = jnp.stack([first_grad, whole[1]], axis=0)[None]
    return (section_outputs, section_gradients, whole[2][None])


def solution(mesh):
    in_specs = (
        P("section", None, None),
        P("section", None, None),
        P("section", None, None),
        P(),
        P(),
        P("section", None, None),
    )
    out_specs = (
        P(("dp", "section"), None, None, None),
        P(("dp", "section"), None, None, None),
        P(("dp", "section"), None, None),
    )
    return jax.shard_map(local, mesh=mesh, in_specs=in_specs, out_specs=out_specs, check_vma=False)
```

profile of v0, /device:TPU:1, one launch (start us, length us, event | category | flops | bytes accessed | tf_op | source)
XLA Modules:
  0.0 102.0 jit_solution(10804402269663658548)
XLA Ops:
  7.2 0.0 copy-start
  7.2 0.0 all-gather.2.cloned.1.call-start
  7.2 1.7 %copy-done = bf16[1,1152,1152]{2,1,0:T(8,128)(2,1)S(1)} copy-done((bf16[1,1152,1152]{2,1,0:T(8,128)(2,1)S(1)}, bf16[1,1152,1152]{2,1,0:T(8,128)(2,1)}, u32[]{:S(2)}) %copy-start) | copy-done | bytes 2654232
  8.9 1.9 %fusion.34 = bf16[48,1152]{1,0:T(8,128)(2,1)S(1)} fusion(bf16[1,1152,1152]{2,1,0:T(8,128)(2,1)S(1)} %copy-done, pred[]{:T(512)S(6)} %eq.11, bf16[1,768,1152]{2,1,0:T(8,128)(2,1)} %param.8, s32[]{:T(128)S(6)} %select_n.97, bf16[1,768,1152]{2,1,0:T(8,128)(2,1)} %param.7), kind=kOutput, calls=%fused_computation.29 | convolution fusion | flops 127678464 | bytes 3098624 | tf_op jit(solution)/shard_map/dot_general | solution.py:30
  10.8 1.3 %collective-permute-start.2 = (bf16[48,1152]{1,0:T(8,128)(2,1)S(1)}, bf16[48,1152]{1,0:T(8,128)(2,1)S(1)}, u32[]{:S(2)}, u32[]{:S(2)}) collective-permute-start(bf16[48,1152]{1,0:T(8,128)(2,1)S(1)} %fusion.34), channel_id=1, source_target_pairs={{32,0},{64,32},{96,64},{128,96},{160,128},{192,160},{224,192},{240... | collective-permute-start | bytes 331784 | tf_op jit(solution)/shard_map/ppermute | solution.py:53
  12.1 1.6 %bitcast_select_fusion = (bf16[48,1152]{1,0:T(8,128)(2,1)S(1)}, bf16[48,1152]{1,0:T(8,128)(2,1)S(1)}) fusion(pred[]{:T(512)S(6)} %eq.11, bf16[1,768,1152]{2,1,0:T(8,128)(2,1)} %param.8, s32[]{:T(128)S(6)} %select_n.97, bf16[1,768,1152]{2,1,0:T(8,128)(2,1)} %param.7, bf16[1,768,1152]{2,1,0:T(8,128)(2,1)} %param.6, bf16[1,1152,1152]{2,1,0:T(8,128)(2,1)S(1)} %copy-done), kind=kOutput, calls=%fused_computation.37 | convolution fusion | flops 127733760 | bytes 3319296 | tf_op jit(solution)/shard_map/dot_general | solution.py:27
  13.8 9.6 %collective-permute-start.1 = (bf16[48,1152]{1,0:T(8,128)(2,1)S(1)}, bf16[48,1152]{1,0:T(8,128)(2,1)S(1)}, u32[]{:S(2)}, u32[]{:S(2)}) collective-permute-start(bf16[48,1152]{1,0:T(8,128)(2,1)S(1)} %get-tuple-element.8), channel_id=1, source_target_pairs={{0,16},{16,0},{32,48},{48,32},{64,80},{80,64},{96,112},{112,96},{1... | collective-permute-start | bytes 331784 | tf_op jit(solution)/shard_map/ppermute | solution.py:54
  23.4 3.1 %collective-permute-start = (bf16[48,1152]{1,0:T(8,128)(2,1)S(1)}, bf16[48,1152]{1,0:T(8,128)(2,1)S(1)}, u32[]{:S(2)}, u32[]{:S(2)}) collective-permute-start(bf16[48,1152]{1,0:T(8,128)(2,1)S(1)} %get-tuple-element.9), channel_id=1, source_target_pairs={{0,32},{32,64},{64,96},{96,128},{128,160},{160,192},{192,224},{224... | collective-permute-start | bytes 331784 | tf_op jit(solution)/shard_map/ppermute | solution.py:52
  26.5 0.0 collective-permute-done.2
  26.5 5.1 %collective-permute-done.1 = bf16[48,1152]{1,0:T(8,128)(2,1)S(1)} collective-permute-done((bf16[48,1152]{1,0:T(8,128)(2,1)S(1)}, bf16[48,1152]{1,0:T(8,128)(2,1)S(1)}, u32[]{:S(2)}, u32[]{:S(2)}) %collective-permute-start.1) | collective-permute-done | bytes 110624 | tf_op jit(solution)/shard_map/ppermute | solution.py:54
  31.6 0.0 collective-permute-done
  31.6 1.6 %fusion.39 = (bf16[1,48,1152]{2,1,0:T(8,128)(2,1)S(1)}, bf16[48,1152]{1,0:T(8,128)(2,1)S(1)}) fusion(bf16[48,1152]{1,0:T(8,128)(2,1)S(1)} %collective-permute-done.1, pred[]{:T(512)S(6)} %eq.11, bf16[48,1152]{1,0:T(8,128)(2,1)S(1)} %collective-permute-done, bf16[768,1152]{1,0:T(8,128)(2,1)} %param.9, s32[]{:T(128)S(6)} %select_n.97, pred[]{:T(512)S(6)} %eq.12, ...), kind=kOutput, calls=%fused_computation.34 | convolution fusion | flops 127899648 | bytes 3652608 | tf_op jit(solution)/shard_map/dot_general | solution.py:27
  33.2 6.5 %collective-permute-start.3 = (bf16[48,1152]{1,0:T(8,128)(2,1)S(1)}, bf16[48,1152]{1,0:T(8,128)(2,1)S(1)}, u32[]{:S(2)}, u32[]{:S(2)}) collective-permute-start(bf16[48,1152]{1,0:T(8,128)(2,1)S(1)} %get-tuple-element.7), channel_id=1, source_target_pairs={{0,16},{16,0},{32,48},{48,32},{64,80},{80,64},{96,112},{112,96},{1... | collective-permute-start | bytes 331784 | tf_op jit(solution)/shard_map/ppermute | solution.py:59
  39.7 1.9 %fusion.29 = bf16[1,48,1152]{2,1,0:T(8,128)(2,1)S(1)} fusion(bf16[1,1152,1152]{2,1,0:T(8,128)(2,1)S(1)} %copy-done, bf16[48,1152]{1,0:T(8,128)(2,1)S(1)} %collective-permute-done.1, pred[]{:T(512)S(6)} %eq.11, bf16[48,1152]{1,0:T(8,128)(2,1)S(1)} %collective-permute-done.2, bf16[768,1152]{1,0:T(8,128)(2,1)} %param.10, s32[]{:T(128)S(6)} %select_n.97, ...), kind=kOutput, calls=%fused_computation.27 | convolution fusion | flops 127789056 | bytes 3320832 | tf_op jit(solution)/shard_map/dot_general | solution.py:30
  41.6 3.7 %collective-permute-done.3 = bf16[48,1152]{1,0:T(8,128)(2,1)S(1)} collective-permute-done((bf16[48,1152]{1,0:T(8,128)(2,1)S(1)}, bf16[48,1152]{1,0:T(8,128)(2,1)S(1)}, u32[]{:S(2)}, u32[]{:S(2)}) %collective-permute-start.3) | collective-permute-done | bytes 110624 | tf_op jit(solution)/shard_map/ppermute | solution.py:59
  45.2 0.8 pad_maximum_fusion
  46.0 0.0 all-gather.2.cloned.1.call-update
  46.0 0.0 copy-start.3
  46.0 0.0 copy-start.4
  46.0 6.6 %fusion.3 = bf16[1,768,1152]{2,1,0:T(8,128)(2,1)} fusion(bf16[1,1152,1152]{2,1,0:T(8,128)(2,1)S(1)} %copy-done, bf16[1,768,1152]{2,1,0:T(8,128)(2,1)} %param.7, bf16[1,768,1152]{2,1,0:T(8,128)(2,1)} %param.6, pred[]{:T(512)S(6)} %eq.11), kind=kOutput, calls=%fused_computation.7 | convolution fusion | flops 2041970688 | bytes 7962625 | tf_op jit(solution)/shard_map/dot_general | solution.py:27
  52.6 0.0 copy-done.3
  52.6 0.0 copy-done.4
  52.6 4.0 %fusion.17 = bf16[1,768,1152]{2,1,0:T(8,128)(2,1)} fusion(bf16[1,1152,1152]{2,1,0:T(8,128)(2,1)S(1)} %copy-done, bf16[1,768,1152]{2,1,0:T(8,128)(2,1)S(1)} %copy-done.3, bf16[1,768,1152]{2,1,0:T(8,128)(2,1)S(1)} %copy-done.4, pred[]{:T(512)S(6)} %eq.11), kind=kOutput, calls=%fused_computation.19 | convolution fusion | flops 2042855424 | bytes 7962625 | tf_op jit(solution)/shard_map/dot_general | solution.py:30
  56.6 30.9 %all-gather.2.cloned.1.call-done = bf16[3,768,1152]{2,1,0:T(8,128)(2,1)} async-done(((bf16[3,48,1152]{2,1,0:T(8,128)(2,1)}), bf16[3,768,1152]{2,1,0:T(8,128)(2,1)}) %all-gather.2.cloned.1.call-update) | async-done | bytes 5308432 | tf_op jit(solution)/shard_map/all_gather | solution.py:61
  87.5 0.0 copy-start.1
  87.5 0.0 copy-start.2
  87.5 4.3 %fusion.54 = (bf16[1,768,1152]{2,1,0:T(8,128)(2,1)}, bf16[1,768,1152]{2,1,0:T(8,128)(2,1)S(1)}, bf16[1,768,1152]{2,1,0:T(8,128)(2,1)S(1)}) fusion(bf16[3,768,1152]{2,1,0:T(8,128)(2,1)} %all-gather.2.cloned.1.call-done), kind=kLoop, calls=%fused_computation.53 | loop fusion | bytes 10616832 | tf_op jit(solution)/shard_map/slice | solution.py:66
  91.8 0.0 copy-done.1
  91.8 0.0 copy-done.2
  91.8 3.3 %maximum_bitcast_fusion = (bf16[1,2,768,1152]{3,2,1,0:T(8,128)(2,1)}, bf16[1,2,768,1152]{3,2,1,0:T(8,128)(2,1)}) fusion(bf16[1,768,1152]{2,1,0:T(8,128)(2,1)S(1)} %get-tuple-element.5, bf16[1,768,1152]{2,1,0:T(8,128)(2,1)S(1)} %copy-done.1, bf16[1,768,1152]{2,1,0:T(8,128)(2,1)S(1)} %get-tuple-element.4, bf16[1,768,1152]{2,1,0:T(8,128)(2,1)S(1)} %copy-done.2), kind=kLoop, calls=%fused_computation.3 | loop fusion | flops 3538944 | bytes 14155776 | tf_op jit(solution)/shard_map/broadcast_in_dim | solution.py:64
Async XLA Ops:
  7.2 1.8 %copy-start = (bf16[1,1152,1152]{2,1,0:T(8,128)(2,1)S(1)}, bf16[1,1152,1152]{2,1,0:T(8,128)(2,1)}, u32[]{:S(2)}) copy-start(bf16[1,1152,1152]{2,1,0:T(8,128)(2,1)} %param.11) | copy-start | bytes 7962628
  7.2 80.3 %all-gather.2.cloned.1.call-start = ((), (), s32[]{:S(2)}) async-start(), calls=%async_computation | async-start | bytes 5640192 | tf_op jit(solution)/shard_map/all_gather | solution.py:61
  10.8 15.7 %collective-permute-start.2 = (bf16[48,1152]{1,0:T(8,128)(2,1)S(1)}, bf16[48,1152]{1,0:T(8,128)(2,1)S(1)}, u32[]{:S(2)}, u32[]{:S(2)}) collective-permute-start(bf16[48,1152]{1,0:T(8,128)(2,1)S(1)} %fusion.34), channel_id=1, source_target_pairs={{32,0},{64,32},{96,64},{128,96},{160,128},{192,160},{224,192},{240... | collective-permute-start | bytes 331784 | tf_op jit(solution)/shard_map/ppermute | solution.py:53
  13.8 17.8 %collective-permute-start.1 = (bf16[48,1152]{1,0:T(8,128)(2,1)S(1)}, bf16[48,1152]{1,0:T(8,128)(2,1)S(1)}, u32[]{:S(2)}, u32[]{:S(2)}) collective-permute-start(bf16[48,1152]{1,0:T(8,128)(2,1)S(1)} %get-tuple-element.8), channel_id=1, source_target_pairs={{0,16},{16,0},{32,48},{48,32},{64,80},{80,64},{96,112},{112,96},{1... | collective-permute-start | bytes 331784 | tf_op jit(solution)/shard_map/ppermute | solution.py:54
  23.4 8.2 %collective-permute-start = (bf16[48,1152]{1,0:T(8,128)(2,1)S(1)}, bf16[48,1152]{1,0:T(8,128)(2,1)S(1)}, u32[]{:S(2)}, u32[]{:S(2)}) collective-permute-start(bf16[48,1152]{1,0:T(8,128)(2,1)S(1)} %get-tuple-element.9), channel_id=1, source_target_pairs={{0,32},{32,64},{64,96},{96,128},{128,160},{160,192},{192,224},{224... | collective-permute-start | bytes 331784 | tf_op jit(solution)/shard_map/ppermute | solution.py:52
  33.2 12.1 %collective-permute-start.3 = (bf16[48,1152]{1,0:T(8,128)(2,1)S(1)}, bf16[48,1152]{1,0:T(8,128)(2,1)S(1)}, u32[]{:S(2)}, u32[]{:S(2)}) collective-permute-start(bf16[48,1152]{1,0:T(8,128)(2,1)S(1)} %get-tuple-element.7), channel_id=1, source_target_pairs={{0,16},{16,0},{32,48},{48,32},{64,80},{80,64},{96,112},{112,96},{1... | collective-permute-start | bytes 331784 | tf_op jit(solution)/shard_map/ppermute | solution.py:59
  46.0 6.6 %copy-start.3 = (bf16[1,768,1152]{2,1,0:T(8,128)(2,1)S(1)}, bf16[1,768,1152]{2,1,0:T(8,128)(2,1)}, u32[]{:S(2)}) copy-start(bf16[1,768,1152]{2,1,0:T(8,128)(2,1)} %param.8) | copy-start | bytes 5308420
  46.0 6.6 %copy-start.4 = (bf16[1,768,1152]{2,1,0:T(8,128)(2,1)S(1)}, bf16[1,768,1152]{2,1,0:T(8,128)(2,1)}, u32[]{:S(2)}) copy-start(bf16[1,768,1152]{2,1,0:T(8,128)(2,1)} %param.7) | copy-start | bytes 5308420
  87.5 4.3 %copy-start.1 = (bf16[1,768,1152]{2,1,0:T(8,128)(2,1)S(1)}, bf16[1,768,1152]{2,1,0:T(8,128)(2,1)}, u32[]{:S(2)}) copy-start(bf16[1,768,1152]{2,1,0:T(8,128)(2,1)} %fusion.3) | copy-start | bytes 5308420
  87.5 4.3 %copy-start.2 = (bf16[1,768,1152]{2,1,0:T(8,128)(2,1)S(1)}, bf16[1,768,1152]{2,1,0:T(8,128)(2,1)}, u32[]{:S(2)}) copy-start(bf16[1,768,1152]{2,1,0:T(8,128)(2,1)} %fusion.17) | copy-start | bytes 5308420
Sparse Core Ops, SparseCore 0:
  46.1 41.3 all-gather.1
where the time goes:
time: 102 us
  waiting for transfers between devices  39.7 us (39%)
  starting transfers between devices  20.6 us (20%)
  matrix products  17.5 us (17%)
  between operations  14.1 us (14%)
  local copies, waits for them, and re-layouts  6.01 us (6%)
  other arithmetic  4.11 us (4%)
    all_gather x1, waiting for transfers between devices, local(): whole = lax.all_gather(parts, 'dp', axis=1, tiled=True)  30.9 us
    dot_general x3, matrix products, times(): return jnp.dot(left, weights, preferred_element_type=jnp.float32)  9.78 us
    ppermute x1, starting transfers between devices, local(): lax.ppermute(jnp.where(is_early, skip_part, cot_part), 'section', mirror)  9.63 us
    dot_general x3, matrix products, times_t(): lax.dot_general(left, weights, (((1,), (1,)), ((), ())), preferred_elemen...  7.76 us
    ppermute x1, starting transfers between devices, local(): lax.ppermute(jnp.where(is_early, second_skip, second_cot), 'section', mir...  6.51 us
    ppermute x1, waiting for transfers between devices, local(): lax.ppermute(jnp.where(is_early, skip_part, cot_part), 'section', mirror)  5.07 us
    slice x1, local copies, waits for them, and re-layouts, local(): return (section_outputs, section_gradients, whole[2][None])  4.3 us
    ppermute x1, waiting for transfers between devices, local(): lax.ppermute(jnp.where(is_early, second_skip, second_cot), 'section', mir...  3.65 us
  transfers between devices with their start and end apart: 5, of which 3 were waited for; matrix products, arithmetic and copies ran while one was open for 14% of the time, Pallas kernels for 0%

commit v1 on v0

--- a/solution.py
+++ b/solution.py
@@ -58,7 +58,9 @@
     second_grad = backward(second_cot, came_mirror)
     arrived = lax.ppermute(jnp.where(is_early, second_skip, second_cot), "section", mirror)
     parts = jnp.stack([second_out, second_grad, arrived], axis=0)
-    whole = lax.all_gather(parts, "dp", axis=1, tiled=True)
+    whole = jnp.concatenate(
+        lax.all_to_all(jnp.stack([parts] * lax.axis_size("dp")), "dp", 0, 0), axis=1
+    )
     first_out, _ = forward(a, held)
     first_grad = backward(cot, held)
     section_outputs = jnp.stack([first_out, whole[0]], axis=0)[None]

time: 102 us -> 135 us (1.32)
  the two profiles are of different devices: /device:TPU:1 before, /device:TPU:61 now
where the time goes in v1:
time: 135 us; the launch traced here: 134 us
  waiting for transfers between devices  83.7 us (62%)
  starting transfers between devices  20 us (15%)
  matrix products  17.6 us (13%)
  local copies, waits for them, and re-layouts  8.82 us (7%)
  other arithmetic  3.39 us (3%)
    all_to_all x1, waiting for transfers between devices, local(): lax.all_to_all(jnp.stack([parts] * lax.axis_size('dp')), 'dp', 0, 0)  69.2 us
    dot_general x3, matrix products, times(): return jnp.dot(left, weights, preferred_element_type=jnp.float32)  9.78 us
    ppermute x1, starting transfers between devices, local(): came_grad = lax.ppermute(grad_part, 'section', back)  7.89 us
    ppermute x1, waiting for transfers between devices, local(): lax.ppermute(jnp.where(is_early, skip_part, cot_part), 'section', mirror)  7.81 us
    dot_general x3, matrix products, times_t(): lax.dot_general(left, weights, (((1,), (1,)), ((), ())), preferred_elemen...  7.77 us
    all_to_all x1, starting transfers between devices, local(): lax.all_to_all(jnp.stack([parts] * lax.axis_size('dp')), 'dp', 0, 0)  7.02 us
    slice x1, local copies, waits for them, and re-layouts, local(): return (section_outputs, section_gradients, whole[2][None])  4.31 us
    ppermute x1, starting transfers between devices, local(): came_out = lax.ppermute(out_part, 'section', ahead)  3.69 us
  transfers between devices with their start and end apart: 5, of which 4 were waited for; matrix products, arithmetic and copies ran while one was open for 10% of the time, Pallas kernels for 0%

profile of v1, /device:TPU:61, one launch (start us, length us, event | category | flops | bytes accessed | tf_op | source)
XLA Modules:
  0.0 134.2 jit_solution(12255954918779760592)
XLA Ops:
  0.6 0.0 copy-start
  0.7 1.7 %copy-done = bf16[1,1152,1152]{2,1,0:T(8,128)(2,1)S(1)} copy-done((bf16[1,1152,1152]{2,1,0:T(8,128)(2,1)S(1)}, bf16[1,1152,1152]{2,1,0:T(8,128)(2,1)}, u32[]{:S(2)}) %copy-start) | copy-done | bytes 2654232
  2.4 1.9 %fusion.34 = bf16[48,1152]{1,0:T(8,128)(2,1)S(1)} fusion(bf16[1,1152,1152]{2,1,0:T(8,128)(2,1)S(1)} %copy-done, pred[]{:T(512)S(6)} %eq.11, bf16[1,768,1152]{2,1,0:T(8,128)(2,1)} %param.8, s32[]{:T(128)S(6)} %select_n.97, bf16[1,768,1152]{2,1,0:T(8,128)(2,1)} %param.7), kind=kOutput, calls=%fused_computation.29 | convolution fusion | flops 127678464 | bytes 3098624 | tf_op jit(solution)/shard_map/dot_general | solution.py:30
  4.3 7.9 %collective-permute-start.2 = (bf16[48,1152]{1,0:T(8,128)(2,1)S(1)}, bf16[48,1152]{1,0:T(8,128)(2,1)S(1)}, u32[]{:S(2)}, u32[]{:S(2)}) collective-permute-start(bf16[48,1152]{1,0:T(8,128)(2,1)S(1)} %fusion.34), channel_id=1, source_target_pairs={{32,0},{64,32},{96,64},{128,96},{160,128},{192,160},{224,192},{240... | collective-permute-start | bytes 331784 | tf_op jit(solution)/shard_map/ppermute | solution.py:53
  12.2 1.6 %bitcast_select_fusion = (bf16[48,1152]{1,0:T(8,128)(2,1)S(1)}, bf16[48,1152]{1,0:T(8,128)(2,1)S(1)}) fusion(pred[]{:T(512)S(6)} %eq.11, bf16[1,768,1152]{2,1,0:T(8,128)(2,1)} %param.8, s32[]{:T(128)S(6)} %select_n.97, bf16[1,768,1152]{2,1,0:T(8,128)(2,1)} %param.7, bf16[1,768,1152]{2,1,0:T(8,128)(2,1)} %param.6, bf16[1,1152,1152]{2,1,0:T(8,128)(2,1)S(1)} %copy-done), kind=kOutput, calls=%fused_computation.37 | convolution fusion | flops 127733760 | bytes 3319296 | tf_op jit(solution)/shard_map/dot_general | solution.py:27
  13.8 1.3 collective-permute-start.1
  15.2 3.7 %collective-permute-start = (bf16[48,1152]{1,0:T(8,128)(2,1)S(1)}, bf16[48,1152]{1,0:T(8,128)(2,1)S(1)}, u32[]{:S(2)}, u32[]{:S(2)}) collective-permute-start(bf16[48,1152]{1,0:T(8,128)(2,1)S(1)} %get-tuple-element.9), channel_id=1, source_target_pairs={{0,32},{32,64},{64,96},{96,128},{128,160},{160,192},{192,224},{224... | collective-permute-start | bytes 331784 | tf_op jit(solution)/shard_map/ppermute | solution.py:52
  18.9 0.0 collective-permute-done.2
  18.9 7.8 %collective-permute-done.1 = bf16[48,1152]{1,0:T(8,128)(2,1)S(1)} collective-permute-done((bf16[48,1152]{1,0:T(8,128)(2,1)S(1)}, bf16[48,1152]{1,0:T(8,128)(2,1)S(1)}, u32[]{:S(2)}, u32[]{:S(2)}) %collective-permute-start.1) | collective-permute-done | bytes 110624 | tf_op jit(solution)/shard_map/ppermute | solution.py:54
  26.7 3.7 %collective-permute-done = bf16[48,1152]{1,0:T(8,128)(2,1)S(1)} collective-permute-done((bf16[48,1152]{1,0:T(8,128)(2,1)S(1)}, bf16[48,1152]{1,0:T(8,128)(2,1)S(1)}, u32[]{:S(2)}, u32[]{:S(2)}) %collective-permute-start) | collective-permute-done | bytes 110624 | tf_op jit(solution)/shard_map/ppermute | solution.py:52
  30.4 1.6 %fusion.39 = (bf16[1,48,1152]{2,1,0:T(8,128)(2,1)S(1)}, bf16[48,1152]{1,0:T(8,128)(2,1)S(1)}) fusion(bf16[48,1152]{1,0:T(8,128)(2,1)S(1)} %collective-permute-done.1, pred[]{:T(512)S(6)} %eq.11, bf16[48,1152]{1,0:T(8,128)(2,1)S(1)} %collective-permute-done, bf16[768,1152]{1,0:T(8,128)(2,1)} %param.9, s32[]{:T(128)S(6)} %select_n.97, pred[]{:T(512)S(6)} %eq.12, ...), kind=kOutput, calls=%fused_computation.34 | convolution fusion | flops 127899648 | bytes 3652608 | tf_op jit(solution)/shard_map/dot_general | solution.py:27
  31.9 0.1 collective-permute-start.3
  32.0 1.9 %fusion.29 = bf16[1,48,1152]{2,1,0:T(8,128)(2,1)S(1)} fusion(bf16[1,1152,1152]{2,1,0:T(8,128)(2,1)S(1)} %copy-done, bf16[48,1152]{1,0:T(8,128)(2,1)S(1)} %collective-permute-done.1, pred[]{:T(512)S(6)} %eq.11, bf16[48,1152]{1,0:T(8,128)(2,1)S(1)} %collective-permute-done.2, bf16[768,1152]{1,0:T(8,128)(2,1)} %param.10, s32[]{:T(128)S(6)} %select_n.97, ...), kind=kOutput, calls=%fused_computation.27 | convolution fusion | flops 127789056 | bytes 3320832 | tf_op jit(solution)/shard_map/dot_general | solution.py:30
  33.9 3.0 %collective-permute-done.3 = bf16[48,1152]{1,0:T(8,128)(2,1)S(1)} collective-permute-done((bf16[48,1152]{1,0:T(8,128)(2,1)S(1)}, bf16[48,1152]{1,0:T(8,128)(2,1)S(1)}, u32[]{:S(2)}, u32[]{:S(2)}) %collective-permute-start.3) | collective-permute-done | bytes 110624 | tf_op jit(solution)/shard_map/ppermute | solution.py:59
  37.0 2.8 %stack.23 = bf16[16,3,48,1152]{3,2,1,0:T(8,128)(2,1)} broadcast(bf16[3,48,1152]{2,1,0:T(8,128)(2,1)S(1)} %pad_maximum_fusion), dimensions={1,2,3} | broadcast | bytes 5640192 | tf_op jit(solution)/shard_map/stack | solution.py:62
  39.8 7.0 %all-to-all-start = ((bf16[16,3,48,1152]{3,2,1,0:T(8,128)(2,1)}), bf16[16,3,48,1152]{3,2,1,0:T(8,128)(2,1)}, u32[]{:S(2)}, u32[]{:S(2)}) async-start(bf16[16,3,48,1152]{3,2,1,0:T(8,128)(2,1)} %stack.23), calls=%async_computation | async-start | bytes 10616832 | tf_op jit(solution)/shard_map/all_to_all | solution.py:62
  46.8 0.0 copy-start.3
  46.8 0.0 copy-start.4
  46.8 6.6 %fusion.3 = bf16[1,768,1152]{2,1,0:T(8,128)(2,1)} fusion(bf16[1,1152,1152]{2,1,0:T(8,128)(2,1)S(1)} %copy-done, bf16[1,768,1152]{2,1,0:T(8,128)(2,1)} %param.7, bf16[1,768,1152]{2,1,0:T(8,128)(2,1)} %param.6, pred[]{:T(512)S(6)} %eq.11), kind=kOutput, calls=%fused_computation.7 | convolution fusion | flops 2041970688 | bytes 7962625 | tf_op jit(solution)/shard_map/dot_general | solution.py:27
  53.4 0.0 copy-done.3
  53.4 0.0 copy-done.4
  53.4 4.0 %fusion.17 = bf16[1,768,1152]{2,1,0:T(8,128)(2,1)} fusion(bf16[1,1152,1152]{2,1,0:T(8,128)(2,1)S(1)} %copy-done, bf16[1,768,1152]{2,1,0:T(8,128)(2,1)S(1)} %copy-done.3, bf16[1,768,1152]{2,1,0:T(8,128)(2,1)S(1)} %copy-done.4, pred[]{:T(512)S(6)} %eq.11), kind=kOutput, calls=%fused_computation.19 | convolution fusion | flops 2042855424 | bytes 7962625 | tf_op jit(solution)/shard_map/dot_general | solution.py:30
  57.4 69.2 %all-to-all-done = bf16[16,3,48,1152]{3,2,1,0:T(8,128)(2,1)} async-done(((bf16[16,3,48,1152]{3,2,1,0:T(8,128)(2,1)}), bf16[16,3,48,1152]{3,2,1,0:T(8,128)(2,1)}, u32[]{:S(2)}, u32[]{:S(2)}) %all-to-all-start) | async-done | bytes 5308448 | tf_op jit(solution)/shard_map/all_to_all | solution.py:62
  126.5 0.0 copy-start.1
  126.5 0.0 copy-start.2
  126.5 4.3 %fusion.54 = (bf16[1,16,48,1152]{3,2,0,1:T(8,128)(2,1)}, bf16[1,16,48,1152]{3,2,0,1:T(8,128)(2,1)S(1)}, bf16[1,16,48,1152]{3,2,0,1:T(8,128)(2,1)S(1)}) fusion(bf16[3,16,48,1152]{3,2,0,1:T(8,128)(2,1)} %bitcast.11), kind=kLoop, calls=%fused_computation.53 | loop fusion | bytes 10616832 | tf_op jit(solution)/shard_map/slice | solution.py:68
  130.8 0.0 copy-done.1
  130.8 0.0 copy-done.2
  130.8 3.3 %maximum_bitcast_fusion = (bf16[1,2,768,1152]{3,2,1,0:T(8,128)(2,1)}, bf16[1,2,768,1152]{3,2,1,0:T(8,128)(2,1)}) fusion(bf16[1,768,1152]{2,1,0:T(8,128)(2,1)S(1)} %bitcast.76, bf16[1,768,1152]{2,1,0:T(8,128)(2,1)S(1)} %copy-done.1, bf16[1,768,1152]{2,1,0:T(8,128)(2,1)S(1)} %bitcast.75, bf16[1,768,1152]{2,1,0:T(8,128)(2,1)S(1)} %copy-done.2), kind=kLoop, calls=%fused_computation.3 | loop fusion | flops 3538944 | bytes 14155776 | tf_op jit(solution)/shard_map/broadcast_in_dim | solution.py:66
  (1 shorter events, 0.0 us)
Async XLA Ops:
  0.6 1.8 %copy-start = (bf16[1,1152,1152]{2,1,0:T(8,128)(2,1)S(1)}, bf16[1,1152,1152]{2,1,0:T(8,128)(2,1)}, u32[]{:S(2)}) copy-start(bf16[1,1152,1152]{2,1,0:T(8,128)(2,1)} %param.11) | copy-start | bytes 7962628
  4.3 14.6 %collective-permute-start.2 = (bf16[48,1152]{1,0:T(8,128)(2,1)S(1)}, bf16[48,1152]{1,0:T(8,128)(2,1)S(1)}, u32[]{:S(2)}, u32[]{:S(2)}) collective-permute-start(bf16[48,1152]{1,0:T(8,128)(2,1)S(1)} %fusion.34), channel_id=1, source_target_pairs={{32,0},{64,32},{96,64},{128,96},{160,128},{192,160},{224,192},{240... | collective-permute-start | bytes 331784 | tf_op jit(solution)/shard_map/ppermute | solution.py:53
  13.8 12.8 %collective-permute-start.1 = (bf16[48,1152]{1,0:T(8,128)(2,1)S(1)}, bf16[48,1152]{1,0:T(8,128)(2,1)S(1)}, u32[]{:S(2)}, u32[]{:S(2)}) collective-permute-start(bf16[48,1152]{1,0:T(8,128)(2,1)S(1)} %get-tuple-element.8), channel_id=1, source_target_pairs={{0,16},{16,0},{32,48},{48,32},{64,80},{80,64},{96,112},{112,96},{1... | collective-permute-start | bytes 331784 | tf_op jit(solution)/shard_map/ppermute | solution.py:54
  15.2 15.2 %collective-permute-start = (bf16[48,1152]{1,0:T(8,128)(2,1)S(1)}, bf16[48,1152]{1,0:T(8,128)(2,1)S(1)}, u32[]{:S(2)}, u32[]{:S(2)}) collective-permute-start(bf16[48,1152]{1,0:T(8,128)(2,1)S(1)} %get-tuple-element.9), channel_id=1, source_target_pairs={{0,32},{32,64},{64,96},{96,128},{128,160},{160,192},{192,224},{224... | collective-permute-start | bytes 331784 | tf_op jit(solution)/shard_map/ppermute | solution.py:52
  31.9 5.0 %collective-permute-start.3 = (bf16[48,1152]{1,0:T(8,128)(2,1)S(1)}, bf16[48,1152]{1,0:T(8,128)(2,1)S(1)}, u32[]{:S(2)}, u32[]{:S(2)}) collective-permute-start(bf16[48,1152]{1,0:T(8,128)(2,1)S(1)} %get-tuple-element.7), channel_id=1, source_target_pairs={{0,16},{16,0},{32,48},{48,32},{64,80},{80,64},{96,112},{112,96},{1... | collective-permute-start | bytes 331784 | tf_op jit(solution)/shard_map/ppermute | solution.py:59
  39.8 86.7 %all-to-all-start = ((bf16[16,3,48,1152]{3,2,1,0:T(8,128)(2,1)}), bf16[16,3,48,1152]{3,2,1,0:T(8,128)(2,1)}, u32[]{:S(2)}, u32[]{:S(2)}) async-start(bf16[16,3,48,1152]{3,2,1,0:T(8,128)(2,1)} %stack.23), calls=%async_computation | async-start | bytes 10616832 | tf_op jit(solution)/shard_map/all_to_all | solution.py:62
  46.8 6.6 %copy-start.3 = (bf16[1,768,1152]{2,1,0:T(8,128)(2,1)S(1)}, bf16[1,768,1152]{2,1,0:T(8,128)(2,1)}, u32[]{:S(2)}) copy-start(bf16[1,768,1152]{2,1,0:T(8,128)(2,1)} %param.8) | copy-start | bytes 5308420
  46.8 6.6 %copy-start.4 = (bf16[1,768,1152]{2,1,0:T(8,128)(2,1)S(1)}, bf16[1,768,1152]{2,1,0:T(8,128)(2,1)}, u32[]{:S(2)}) copy-start(bf16[1,768,1152]{2,1,0:T(8,128)(2,1)} %param.7) | copy-start | bytes 5308420
  126.5 4.3 %copy-start.1 = (bf16[1,768,1152]{2,1,0:T(8,128)(2,1)S(1)}, bf16[1,768,1152]{2,1,0:T(8,128)(2,1)}, u32[]{:S(2)}) copy-start(bf16[1,768,1152]{2,1,0:T(8,128)(2,1)} %fusion.3) | copy-start | bytes 5308420
  126.5 4.3 %copy-start.2 = (bf16[1,768,1152]{2,1,0:T(8,128)(2,1)S(1)}, bf16[1,768,1152]{2,1,0:T(8,128)(2,1)}, u32[]{:S(2)}) copy-start(bf16[1,768,1152]{2,1,0:T(8,128)(2,1)} %fusion.17) | copy-start | bytes 5308420
